TPU v7x, 32 devices: a whole 2x2x4 slice. The times are simulated.
32 devices in a mesh: req: 4 (over z), mlp: 8 (over y, x, core).
Axes of the slice: x: 2, y: 2, z: 4, core: 2. Of those that a mesh axis runs over, the one named last changes fastest.
Arguments:
- tokens: bfloat16 [1024, 5120], P(('req', 'mlp')), may hold values from -6 to 6
- modulation: float32 [16, 6, 5120], P('req'), may hold values from -3 to 3
- lengths: int32 [4, 4], P('req'), may hold values from 1 to 160, 256 in all within a row
- request_adapter: int32 [16], P('req'), may hold values from 0 to 31
- adapter_storage: int32 [32], replicated, may hold values from 0 to 31, each once
- adapter_down_weight: bfloat16 [32, 5120, 32], P('mlp'), may hold values from -0.078125 to 0.078125
- adapter_up_maps: bfloat16 [32, 2, 16, 4096], P('mlp'), may hold values from -1.5 to 1.5
- input_projection: bfloat16 [4, 5120, 4096], P(None, None, 'mlp'), may hold values from -0.078125 to 0.078125
- query_key_gains: float32 [3, 4096], P(None, 'mlp'), may hold values from 0.1 to 1.9
- positions: int32 [3, 1024], P(None, 'req'), may hold values from 0 to 63
- block_page_lookup: int32 [4, 16], P('req'), may hold values from 0 to 15, each once within a row
- output_projection: bfloat16 [2, 4096, 5120], P(None, 'mlp'), may hold values from -0.09375 to 0.09375
- cross_norm_gain: float32 [5120], replicated, may hold values from 0.1 to 1.9
- text_token_cache: bfloat16 [2, 16, 512, 4096], P(None, 'req', None, 'mlp'), may hold values from -3 to 3
- feedforward_up: bfloat16 [5120, 8192], P('req', 'mlp'), may hold values from -0.078125 to 0.078125
- feedforward_down: bfloat16 [8192, 5120], P('mlp', 'req'), may hold values from -0.0625 to 0.0625
Outputs:
- layer_out: bfloat16 [1024, 5120], P(('req', 'mlp'))
- kv_pages: bfloat16 [2, 64, 16, 4096], P(None, 'req', None, 'mlp')
Inputs may be any that keep to these rules, and one draw needn't show every extreme that they name: `lengths`: row g lists the token counts of the 4 requests of group g in order; they fill the group's 256 positions, and the largest is 160. A permutation: adapter a is stored at index adapter_storage[a] of adapter_down_weight and adapter_up_maps. `block_page_lookup`: each row is a permutation of a group's 16 pages.
All inputs are finite; a program needn't handle non-finite values.
Results may differ from a plain program's by a relative error of at most 0.017.
Values may be sent and summed in bfloat16 or wider, within the bound.
A program may use at most 192 MiB of HBM per device.

v0:
```python
import math
import jax
import jax.numpy as jnp
from jax import lax
from jax.sharding import PartitionSpec as P

HD = 128
PAGE = 16
EPSILON = 1e-06


def as_sent(array):

    def short(part):
        return part.astype(jnp.bfloat16) if part.dtype == jnp.float32 else part

    return jax.tree.map(short, array)


def layer_norm(values):
    center = values - jnp.mean(values, axis=-1, keepdims=True)
    spread = jnp.mean(center * center, axis=-1, keepdims=True)
    return center * lax.rsqrt(spread + EPSILON)


def rotary_tables(grid):
    half_dim = HD // 2
    spatial = half_dim // 3
    temporal = half_dim - 2 * spatial
    column = jnp.arange(half_dim, dtype=jnp.int32)
    which_axis = jnp.where(
        column < temporal, 0, jnp.where(column < temporal + spatial, 1, 2)
    ).astype(jnp.int32)
    offset = jnp.where(
        which_axis == 0, 0, jnp.where(which_axis == 1, temporal, temporal + spatial)
    ).astype(jnp.int32)
    span_size = jnp.where(which_axis == 0, temporal, spatial).astype(jnp.float32)
    frequency = jnp.exp(-(column - offset).astype(jnp.float32) / span_size * math.log(10000.0))
    coordinate = grid.astype(jnp.float32)[which_axis, :].T
    angles = coordinate * frequency[None, :]
    return (jnp.cos(angles), jnp.sin(angles))


def rotate(values, cosine, sine_part):
    half_dim = HD // 2
    front_half = values[..., :half_dim]
    back_half = values[..., half_dim:]
    cosine = cosine[:, None, :]
    sine_part = sine_part[:, None, :]
    return jnp.concatenate(
        [front_half * cosine - back_half * sine_part, back_half * cosine + front_half * sine_part],
        axis=-1,
    )


def attend(queries, key_rows, value_rows, allowed):
    scores = jnp.einsum(
        "thd,shd->hts", queries, key_rows, preferred_element_type=jnp.float32
    ) / math.sqrt(HD)
    scores = jnp.where(allowed[None], scores, -1e30)
    weights = jnp.exp(scores)
    weights = (weights / jnp.sum(weights, axis=-1, keepdims=True)).astype(jnp.bfloat16)
    return jnp.einsum(
        "hts,shd->thd", weights, value_rows, preferred_element_type=jnp.float32
    ).astype(jnp.bfloat16)


def choose_rows(table, segment):
    chosen = jnp.zeros((segment.shape[0],) + table.shape[1:], table.dtype)
    for request in range(table.shape[0]):
        picked = (segment == request).reshape((-1,) + (1,) * (table.ndim - 1))
        chosen = jnp.where(picked, table[request][None], chosen)
    return chosen


def body(
    tokens,
    modulation,
    lengths,
    request_adapter,
    adapter_storage,
    adapter_down_weight,
    adapter_up_maps,
    input_projection,
    query_key_gains,
    positions,
    block_page_lookup,
    output_projection,
    cross_norm_gain,
    text_token_cache,
    feedforward_up,
    feedforward_down,
):
    mlp_count = lax.axis_size("mlp")
    my_index = lax.axis_index("mlp")
    own_count = tokens.shape[0]
    group_rows = own_count * mlp_count
    local_width = input_projection.shape[2]
    heads_local = local_width // HD
    entire_width = local_width * mlp_count
    resident_slots = adapter_down_weight.shape[0]
    doubled_rank = adapter_down_weight.shape[2]
    rank_once = doubled_rank // 2

    def over_group(own_rows, row_fn):
        return row_fn(lax.all_gather(own_rows, "mlp", axis=0, tiled=True), jnp.int32(0))

    def sum_rows(term_fn):
        return lax.psum_scatter(
            term_fn(jnp.int32(0), own_count * lax.axis_size("mlp")).astype(jnp.bfloat16),
            "mlp",
            scatter_dimension=0,
            tiled=True,
        ).astype(jnp.float32)

    def global_sum(pieces):
        return jax.tree.map(lambda part: part.astype(jnp.float32), lax.psum(as_sent(pieces), "mlp"))

    up_full, down_full = (
        lax.all_gather(feedforward_up, "req", axis=0, tiled=True),
        lax.all_gather(feedforward_down, "req", axis=1, tiled=True),
    )
    adapter_up_weight = lax.all_to_all(
        adapter_up_maps, "mlp", split_axis=3, concat_axis=0, tiled=True
    )
    slot_total = adapter_up_weight.shape[0]
    bounds = jnp.cumsum(lengths[0])
    position = jnp.arange(group_rows, dtype=jnp.int32)
    segment = jnp.sum((position[:, None] >= bounds[None, :]).astype(jnp.int32), axis=1)
    own_start = my_index * own_count
    own_segment = lax.dynamic_slice_in_dim(segment, own_start, own_count)
    per_token = [choose_rows(modulation[:, which_row, :], own_segment) for which_row in range(6)]
    token_f32 = tokens.astype(jnp.float32)
    normed_in = (layer_norm(token_f32) * (1.0 + per_token[1]) + per_token[0]).astype(jnp.bfloat16)

    def project_rows(incoming_rows, row_start):
        row_total = incoming_rows.shape[0]
        parts = [
            jnp.dot(incoming_rows, input_projection[which_map], preferred_element_type=jnp.float32)
            for which_map in range(3)
        ]
        code_block = jnp.einsum(
            "lf,sfe->lse", incoming_rows, adapter_down_weight, preferred_element_type=jnp.float32
        )
        parts.append(code_block.reshape(row_total, resident_slots * doubled_rank))
        return jnp.concatenate(parts, axis=1)

    projected = over_group(normed_in, project_rows)
    query_base = projected[:, :local_width]
    key_linear = projected[:, local_width : 2 * local_width]
    value_base = projected[:, 2 * local_width : 3 * local_width]
    code_block = projected[:, 3 * local_width :].reshape(group_rows, resident_slots, doubled_rank)
    request_slot = adapter_storage[request_adapter]
    token_slot = choose_rows(request_slot, segment)
    held = (
        token_slot[:, None]
        == my_index * resident_slots + jnp.arange(resident_slots, dtype=jnp.int32)[None, :]
    ).astype(jnp.float32)
    my_codes = jnp.sum(held[:, :, None] * code_block, axis=1)
    codes = global_sum(my_codes).astype(jnp.bfloat16)
    everywhere = (token_slot[:, None] == jnp.arange(slot_total, dtype=jnp.int32)[None, :]).astype(
        jnp.float32
    )

    def spread(code_part):
        return (
            (everywhere[:, :, None] * code_part[:, None, :].astype(jnp.float32))
            .reshape(group_rows, slot_total * rank_once)
            .astype(jnp.bfloat16)
        )

    query_up_weight = adapter_up_weight[:, 0].reshape(slot_total * rank_once, local_width)
    value_up_weight = adapter_up_weight[:, 1].reshape(slot_total * rank_once, local_width)
    query_linear = query_base + jnp.dot(
        spread(codes[:, :rank_once]), query_up_weight, preferred_element_type=jnp.float32
    )
    value_rows = (
        value_base
        + jnp.dot(spread(codes[:, rank_once:]), value_up_weight, preferred_element_type=jnp.float32)
    ).astype(jnp.bfloat16)
    query_square, key_square = global_sum(
        (jnp.sum(query_linear * query_linear, axis=1), jnp.sum(key_linear * key_linear, axis=1))
    )
    query_norm = (
        query_linear
        * lax.rsqrt(query_square / entire_width + EPSILON)[:, None]
        * query_key_gains[0]
    )
    key_norm = (
        key_linear * lax.rsqrt(key_square / entire_width + EPSILON)[:, None] * query_key_gains[1]
    )
    cosine, sine_part = rotary_tables(positions)
    query_rot = rotate(query_norm.reshape(group_rows, heads_local, HD), cosine, sine_part).astype(
        jnp.bfloat16
    )
    key_rot = rotate(key_norm.reshape(group_rows, heads_local, HD), cosine, sine_part).astype(
        jnp.bfloat16
    )
    value_heads = value_rows.reshape(group_rows, heads_local, HD)
    page_count = group_rows // PAGE
    stacked = jnp.stack(
        [
            key_rot.reshape(page_count, PAGE, local_width),
            value_rows.reshape(page_count, PAGE, local_width),
        ]
    )
    kv_pages = jnp.zeros_like(stacked).at[:, block_page_lookup[0]].set(stacked)
    allowed = segment[:, None] == segment[None, :]
    attended = attend(query_rot, key_rot, value_heads, allowed).reshape(group_rows, local_width)
    text_owner = (
        jnp.arange(text_token_cache.shape[1] * text_token_cache.shape[2], dtype=jnp.int32)
        // text_token_cache.shape[2]
    )
    cross_allowed = segment[:, None] == text_owner[None, :]
    text_keys = text_token_cache[0].reshape(-1, heads_local, HD)
    text_values = text_token_cache[1].reshape(-1, heads_local, HD)

    def attend_term(row_start, row_total):
        return jnp.dot(attended, output_projection[0], preferred_element_type=jnp.float32)

    first_res = (token_f32 + per_token[2] * sum_rows(attend_term)).astype(jnp.bfloat16)
    cross_own = (layer_norm(first_res.astype(jnp.float32)) * cross_norm_gain).astype(jnp.bfloat16)

    def cross_rows(incoming_rows, row_start):
        return jnp.dot(incoming_rows, input_projection[3], preferred_element_type=jnp.float32)

    cross_linear = over_group(cross_own, cross_rows)
    cross_square = global_sum(jnp.sum(cross_linear * cross_linear, axis=1))
    cross_query = (
        cross_linear
        * lax.rsqrt(cross_square / entire_width + EPSILON)[:, None]
        * query_key_gains[2]
    ).astype(jnp.bfloat16)
    cross_out = attend(
        cross_query.reshape(group_rows, heads_local, HD), text_keys, text_values, cross_allowed
    ).reshape(group_rows, local_width)

    def cross_term(row_start, row_total):
        return jnp.dot(cross_out, output_projection[1], preferred_element_type=jnp.float32)

    second_res = (first_res.astype(jnp.float32) + sum_rows(cross_term)).astype(jnp.bfloat16)
    mlp_own = (
        layer_norm(second_res.astype(jnp.float32)) * (1.0 + per_token[4]) + per_token[3]
    ).astype(jnp.bfloat16)

    def expand_rows(incoming_rows, row_start):
        return jax.nn.gelu(
            jnp.dot(incoming_rows, up_full, preferred_element_type=jnp.float32), approximate=True
        ).astype(jnp.bfloat16)

    hidden = over_group(mlp_own, expand_rows)

    def down_term(row_start, row_total):
        return jnp.dot(hidden, down_full, preferred_element_type=jnp.float32)

    layer_out = (second_res.astype(jnp.float32) + per_token[5] * sum_rows(down_term)).astype(
        jnp.bfloat16
    )
    return (layer_out, kv_pages)


def solution(mesh):
    return jax.shard_map(
        body,
        mesh=mesh,
        in_specs=(
            P(("req", "mlp"), None),
            P("req", None, None),
            P("req", None),
            P("req"),
            P(),
            P("mlp", None, None),
            P("mlp", None, None, None),
            P(None, None, "mlp"),
            P(None, "mlp"),
            P(None, "req"),
            P("req", None),
            P(None, "mlp", None),
            P(),
            P(None, "req", None, "mlp"),
            P("req", "mlp"),
            P("mlp", "req"),
        ),
        out_specs=(P(("req", "mlp"), None), P(None, "req", None, "mlp")),
        check_vma=False,
    )
```

profile of v0, /device:TPU:0, one launch (start us, length us, event | category | flops | bytes accessed | tf_op | source)
XLA Modules:
  0.0 720.8 jit_solution(13914493310342817437)
XLA Ops:
  8.1 2.6 fusion.93
  10.7 0.8 reduce-window.8
  11.7 1.1 convert_reduce_fusion.2
  12.9 1.2 fusion.48
  14.1 2.1 fusion.51
  16.2 11.0 %copy.88 = bf16[4,2,16,4096]{2,0,1,3:T(4,128)(2,1)} copy(bf16[4,2,16,4096]{3,2,1,0:T(8,128)(2,1)} %param.22) | data formatting | bytes 2097152 | tf_op args[6]
  27.2 11.3 %reshape.439 = bf16[8,2,32768]{2,1,0:T(2,128)(2,1)} reshape(bf16[4096,2,4,16]{3,2,1,0:T(4,128)(2,1)} %bitcast.123) | data formatting | bytes 2097152
  38.5 5.2 all-to-all-start
  45.1 0.7 fusion.96
  45.8 2.5 compare_select_fusion.10
  48.7 0.8 copy.94
  50.8 0.7 broadcast_compare_fusion.1
  51.5 8.3 %all-to-all-done = bf16[8,2,32768]{2,1,0:T(2,128)(2,1)S(1)} async-done(((bf16[8,2,32768]{2,1,0:T(2,128)(2,1)}), bf16[8,2,32768]{2,1,0:T(2,128)(2,1)S(1)}, u32[]{:S(2)}, u32[]{:S(2)}) %all-to-all-start) | async-done | bytes 1048608 | tf_op jit(solution)/shard_map/all_to_all | solution.py:123
  59.8 7.6 %reshape.440 = bf16[4096,2,4,16]{3,2,1,0:T(4,128)(2,1)} reshape(bf16[8,2,32768]{2,1,0:T(2,128)(2,1)S(1)} %all-to-all-done) | data formatting | bytes 2097152
  67.3 10.8 %copy.106 = bf16[4,2,16,8,512]{4,2,1,0,3:T(8,128)(2,1)S(1)} copy(bf16[4,2,16,8,512]{2,0,1,4,3:T(4,128)(2,1)} %bitcast.122) | data formatting | bytes 2097152 | tf_op jit(solution)/shard_map/all_to_all | solution.py:123
  78.2 2.7 fusion.99
  81.0 22.3 %psum.28 = bf16[256,32]{0,1:T(8,128)(2,1)S(1)} all-reduce(bf16[256,32]{0,1:T(8,128)(2,1)S(1)} %multiply_reduce_fusion.3), channel_id=1, replica_groups=mesh['req'=4,'mlp'=8] {'mlp'}, use_global_device_ids=true, to_apply=%region_5.6 | all-reduce | flops 8192 | bytes 32768 | tf_op jit(solution)/shard_map/psum | solution.py:117
  103.3 1.6 multiply_convert_fusion.1
  104.9 4.9 fusion.7
  110.3 4.1 multiply_reduce_fusion.1
  114.4 12.0 %all-reduce = (bf16[256]{0:T(256)(128)(2,1)S(1)}, bf16[256]{0:T(256)(128)(2,1)S(1)}) all-reduce(bf16[256]{0:T(256)(128)(2,1)S(1)} %get-tuple-element.62, bf16[256]{0:T(256)(128)(2,1)S(1)} %get-tuple-element.64), channel_id=1, replica_groups=mesh['req'=4,'mlp'=8] {'mlp'}, use_global_device_ids=true, to_apply=%region_9.10 | all-reduce | flops 512 | bytes 2048 | tf_op jit(solution)/shard_map/psum | solution.py:117
  127.7 4.8 fusion.9
  132.9 0.8 copy.107
  134.7 1.3 convolution_convert_fusion.3
  136.1 5.6 convolution_convert_fusion.2
  141.7 1.2 fusion.94
  142.9 42.6 %reduce-scatter.4.cloned.1.call-done = bf16[32,5120]{1,0:T(8,128)(2,1)} async-done(((bf16[256,5120]{1,0:T(8,128)(2,1)}), bf16[32,5120]{1,0:T(8,128)(2,1)}) %reduce-scatter.4.cloned.1.call-update) | async-done | bytes 327696 | tf_op jit(solution)/shard_map/reduce_scatter | solution.py:109
  185.5 1.4 convert_reduce_fusion.1
  187.1 0.9 fusion.47
  188.1 4.0 fusion.89
  192.1 4.0 reshape_squeeze.14
  196.1 2.1 reshape.438
  198.6 19.7 %all-gather.8.cloned.1.call-done = bf16[256,5120]{1,0:T(8,128)(2,1)} async-done(((bf16[32,5120]{1,0:T(8,128)(2,1)}), bf16[256,5120]{1,0:T(8,128)(2,1)}) %all-gather.8.cloned.1.call-update) | async-done | bytes 2621456 | tf_op jit(solution)/shard_map/all_gather | solution.py:106
  218.3 5.6 multiply_reduce_fusion
  223.9 13.3 %psum.31 = bf16[256]{0:T(256)(128)(2,1)S(1)} all-reduce(bf16[256]{0:T(256)(128)(2,1)S(1)} %get-tuple-element.66), channel_id=1, replica_groups=mesh['req'=4,'mlp'=8] {'mlp'}, use_global_device_ids=true, to_apply=%region_15.16 | all-reduce | flops 256 | bytes 1024 | tf_op jit(solution)/shard_map/psum | solution.py:117
  237.3 6.4 fusion
  243.6 5.9 fusion.24
  249.6 3.1 convolution_convert_fusion.1
  254.0 42.6 %reduce-scatter.6.cloned.1.call-done = bf16[32,5120]{1,0:T(8,128)(2,1)} async-done(((bf16[256,5120]{1,0:T(8,128)(2,1)}), bf16[32,5120]{1,0:T(8,128)(2,1)}) %reduce-scatter.6.cloned.1.call-update) | async-done | bytes 327696 | tf_op jit(solution)/shard_map/reduce_scatter | solution.py:109
  296.6 1.2 convert_reduce_fusion
  298.1 1.1 fusion.44
  299.6 139.0 %all-gather.12.cloned.1.call-done = bf16[5120,1024]{1,0:T(8,128)(2,1)} async-done(((bf16[1280,1024]{1,0:T(8,128)(2,1)}), bf16[5120,1024]{1,0:T(8,128)(2,1)}) %all-gather.12.cloned.1.call-update) | async-done | bytes 10485776 | tf_op jit(solution)/shard_map/all_gather | solution.py:120
  438.6 183.4 %all-gather.14.cloned.1.call-done = bf16[1024,5120]{1,0:T(8,128)(2,1)} async-done(((bf16[1024,1280]{1,0:T(8,128)(2,1)}), bf16[1024,5120]{1,0:T(8,128)(2,1)}) %all-gather.14.cloned.1.call-update) | async-done | bytes 10485776 | tf_op jit(solution)/shard_map/all_gather | solution.py:121
  622.0 30.5 %all-gather.10.cloned.1.call-done = bf16[256,5120]{1,0:T(8,128)(2,1)} async-done(((bf16[32,5120]{1,0:T(8,128)(2,1)}), bf16[256,5120]{1,0:T(8,128)(2,1)}) %all-gather.10.cloned.1.call-update) | async-done | bytes 2621456 | tf_op jit(solution)/shard_map/all_gather | solution.py:106
  652.5 15.1 %convolution_convert_fusion = bf16[256,5120]{1,0:T(8,128)(2,1)} fusion(bf16[1024,5120]{1,0:T(8,128)(2,1)} %all-gather.14.cloned.1.call-done, bf16[256,5120]{1,0:T(8,128)(2,1)} %all-gather.10.cloned.1.call-done, bf16[5120,1024]{1,0:T(8,128)(2,1)} %all-gather.12.cloned.1.call-done), kind=kOutput, calls=%fused_computation.6 | convolution fusion | flops 5372379136 | bytes 26214400 | tf_op jit(solution)/shard_map/dot_general | solution.py:254
  668.2 1.2 scatter_fusion
  669.5 42.0 %reduce-scatter.8.cloned.1.call-done = bf16[32,5120]{1,0:T(8,128)(2,1)} async-done(((bf16[256,5120]{1,0:T(8,128)(2,1)}), bf16[32,5120]{1,0:T(8,128)(2,1)}) %reduce-scatter.8.cloned.1.call-update) | async-done | bytes 327696 | tf_op jit(solution)/shard_map/reduce_scatter | solution.py:109
  711.5 2.0 fusion.54
  (150 shorter events, 9.5 us)
Async XLA Ops:
  8.0 70.2 %copy-start = (bf16[4,5120,32]{1,2,0:T(8,128)(2,1)S(1)}, bf16[4,5120,32]{1,2,0:T(8,128)(2,1)}, u32[]{:S(2)}) copy-start(bf16[4,5120,32]{1,2,0:T(8,128)(2,1)} %param.21) | copy-start | bytes 3932164
  8.0 70.2 %all-gather.6.cloned.1.call-start = ((), (), s32[]{:S(2)}) async-start(), calls=%async_computation.4 | async-start | bytes 2949120 | tf_op jit(solution)/shard_map/all_gather | solution.py:106
  11.7 15.5 %copy-start.27 = (pred[32]{0:T(512)(128)(4,1)}, pred[32]{0:T(512)(128)(4,1)S(1)}, u32[]{:S(2)}) copy-start(pred[32]{0:T(512)(128)(4,1)S(1)} %get-tuple-element.60) | copy-start | bytes 100
  11.7 15.5 %copy-start.29 = (pred[32]{0:T(512)(128)(4,1)}, pred[32]{0:T(512)(128)(4,1)S(1)}, u32[]{:S(2)}) copy-start(pred[32]{0:T(512)(128)(4,1)S(1)} %get-tuple-element.61) | copy-start | bytes 100
  27.2 16.5 %copy-start.34 = (s32[3,256]{1,0:T(4,128)S(1)}, s32[3,256]{1,0:T(4,128)}, u32[]{:S(2)}) copy-start(s32[3,256]{1,0:T(4,128)} %param.25) | copy-start | bytes 9220
  27.2 16.6 %copy-start.36 = (s32[4]{0:T(128)S(1)}, s32[4]{0:T(128)}, u32[]{:S(2)}) copy-start(s32[4]{0:T(128)} %param.19) | copy-start | bytes 52
  27.2 16.6 %copy-start.2 = (s32[32]{0:T(128)S(1)}, s32[32]{0:T(128)}, u32[]{:S(2)}) copy-start(s32[32]{0:T(128)} %param.20) | copy-start | bytes 388
  27.2 22.4 %copy-start.33 = (f32[3,512]{1,0:T(4,128)S(1)}, f32[3,512]{1,0:T(4,128)}, u32[]{:S(2)}) copy-start(f32[3,512]{1,0:T(4,128)} %param.24) | copy-start | bytes 18436
  38.5 21.3 %all-to-all-start = ((bf16[8,2,32768]{2,1,0:T(2,128)(2,1)}), bf16[8,2,32768]{2,1,0:T(2,128)(2,1)S(1)}, u32[]{:S(2)}, u32[]{:S(2)}) async-start(bf16[8,2,32768]{2,1,0:T(2,128)(2,1)} %reshape.439), calls=%async_computation | async-start | bytes 2097152 | tf_op jit(solution)/shard_map/all_to_all | solution.py:123
  43.7 141.8 %reduce-scatter.4.cloned.1.call-start = ((), (), s32[]{:S(2)}) async-start(), calls=%async_computation.5 | async-start | bytes 2949120 | tf_op jit(solution)/shard_map/reduce_scatter | solution.py:109
  104.9 5.3 copy-start.4
  110.3 16.2 %copy-start.32 = (f32[1,512]{1,0:T(1,128)S(1)}, f32[1,512]{1,0:T(1,128)}, u32[]{:S(2)}) copy-start(f32[1,512]{1,0:T(1,128)} %get-tuple-element.54) | copy-start | bytes 6148
  110.3 16.8 %copy-start.31 = (f32[1,512]{1,0:T(1,128)S(1)}, f32[1,512]{1,0:T(1,128)}, u32[]{:S(2)}) copy-start(f32[1,512]{1,0:T(1,128)} %get-tuple-element.53) | copy-start | bytes 6148
  127.7 4.9 copy-start.13
  127.7 6.1 copy-start.12
  132.9 3.1 copy-start.5
  136.0 49.5 %copy-start.3 = (bf16[32,5120]{1,0:T(8,128)(2,1)S(1)}, bf16[32,5120]{1,0:T(8,128)(2,1)}, u32[]{:S(2)}) copy-start(bf16[32,5120]{1,0:T(8,128)(2,1)} %param.16) | copy-start | bytes 983044
  136.0 49.4 %copy-start.25 = (f32[1,1,5120]{2,0,1:T(1,128)S(1)}, f32[1,1,5120]{2,0,1:T(1,128)}, u32[]{:S(2)}) copy-start(f32[1,1,5120]{2,0,1:T(1,128)} %get-tuple-element.40) | copy-start | bytes 61444
  136.0 49.4 %copy-start.28 = (pred[32]{0:T(512)(128)(4,1)S(1)}, pred[32]{0:T(512)(128)(4,1)}, u32[]{:S(2)}) copy-start(pred[32]{0:T(512)(128)(4,1)} %copy-done.27) | copy-start | bytes 100
  136.0 49.4 %copy-start.30 = (pred[32]{0:T(512)(128)(4,1)S(1)}, pred[32]{0:T(512)(128)(4,1)}, u32[]{:S(2)}) copy-start(pred[32]{0:T(512)(128)(4,1)} %copy-done.29) | copy-start | bytes 100
  136.1 51.1 %copy-start.26 = (f32[5120]{0:T(1024)S(1)}, f32[5120]{0:T(1024)}, u32[]{:S(2)}) copy-start(f32[5120]{0:T(1024)} %param.28) | copy-start | bytes 61444
  141.7 76.6 %all-gather.8.cloned.1.call-start = ((), (), s32[]{:S(2)}) async-start(), calls=%async_computation.6 | async-start | bytes 2949120 | tf_op jit(solution)/shard_map/all_gather | solution.py:106
  188.1 108.6 %reduce-scatter.6.cloned.1.call-start = ((), (), s32[]{:S(2)}) async-start(), calls=%async_computation.7 | async-start | bytes 2949120 | tf_op jit(solution)/shard_map/reduce_scatter | solution.py:109
  198.6 38.6 %copy-start.10 = (bf16[2048,4,128]{2,1,0:T(4,128)(2,1)S(1)}, bf16[2048,4,128]{2,1,0:T(4,128)(2,1)}, u32[]{:S(2)}) copy-start(bf16[2048,4,128]{2,1,0:T(4,128)(2,1)} %reshape_squeeze.14) | copy-start | bytes 6291460
  198.6 38.6 %copy-start.35 = (f32[1,512]{1,0:T(1,128)S(1)}, f32[1,512]{1,0:T(1,128)}, u32[]{:S(2)}) copy-start(f32[1,512]{1,0:T(1,128)} %get-tuple-element.52) | copy-start | bytes 6148
  237.2 6.4 copy-start.9
  237.2 12.3 %slice-start = ((s8[10485760]{0:T(1024)(128)(4,1)}), s8[4194304]{0:T(1024)(128)(4,1)S(1)}, s32[]{:S(2)}) async-start(s8[10485760]{0:T(1024)(128)(4,1)} %bitcast.159), calls=%async_computation.12 | async-start | bytes 8388608
  243.6 5.9 slice-start.1
  243.6 5.9 slice-start.2
  252.7 45.3 %copy-start.15 = (f32[1,1,5120]{2,0,1:T(1,128)S(1)}, f32[1,1,5120]{2,0,1:T(1,128)}, u32[]{:S(2)}) copy-start(f32[1,1,5120]{2,0,1:T(1,128)} %get-tuple-element.23) | copy-start | bytes 61444
  252.7 45.3 %copy-start.16 = (f32[1,1,5120]{2,0,1:T(1,128)S(1)}, f32[1,1,5120]{2,0,1:T(1,128)}, u32[]{:S(2)}) copy-start(f32[1,1,5120]{2,0,1:T(1,128)} %get-tuple-element.24) | copy-start | bytes 61444
  252.7 45.4 %copy-start.17 = (f32[1,1,5120]{2,0,1:T(1,128)S(1)}, f32[1,1,5120]{2,0,1:T(1,128)}, u32[]{:S(2)}) copy-start(f32[1,1,5120]{2,0,1:T(1,128)} %get-tuple-element.25) | copy-start | bytes 61444
  252.7 45.4 %copy-start.18 = (f32[1,1,5120]{2,0,1:T(1,128)S(1)}, f32[1,1,5120]{2,0,1:T(1,128)}, u32[]{:S(2)}) copy-start(f32[1,1,5120]{2,0,1:T(1,128)} %get-tuple-element.26) | copy-start | bytes 61444
  252.8 45.4 %copy-start.19 = (f32[1,1,5120]{2,0,1:T(1,128)S(1)}, f32[1,1,5120]{2,0,1:T(1,128)}, u32[]{:S(2)}) copy-start(f32[1,1,5120]{2,0,1:T(1,128)} %get-tuple-element.27) | copy-start | bytes 61444
  252.8 45.4 %copy-start.20 = (f32[1,1,5120]{2,0,1:T(1,128)S(1)}, f32[1,1,5120]{2,0,1:T(1,128)}, u32[]{:S(2)}) copy-start(f32[1,1,5120]{2,0,1:T(1,128)} %get-tuple-element.28) | copy-start | bytes 61444
  252.8 185.8 %all-gather.12.cloned.1.call-start = ((), (), s32[]{:S(2)}) async-start(), calls=%async_computation.9 | async-start | bytes 13107200 | tf_op jit(solution)/shard_map/all_gather | solution.py:120
  253.4 368.7 %all-gather.14.cloned.1.call-start = ((), (), s32[]{:S(2)}) async-start(), calls=%async_computation.10 | async-start | bytes 13107200 | tf_op jit(solution)/shard_map/all_gather | solution.py:121
  254.0 398.6 %all-gather.10.cloned.1.call-start = ((), (), s32[]{:S(2)}) async-start(), calls=%async_computation.8 | async-start | bytes 2949120 | tf_op jit(solution)/shard_map/all_gather | solution.py:106
  299.3 368.4 %copy-start.37 = (s32[1,16]{1,0:T(1,128)S(1)}, s32[1,16]{1,0:T(1,128)}, u32[]{:S(2)}) copy-start(s32[1,16]{1,0:T(1,128)} %param.26) | copy-start | bytes 196
  299.3 368.4 %copy-start.8 = (bf16[256,4,128]{2,0,1:T(8,128)(2,1)S(1)}, bf16[256,4,128]{2,0,1:T(8,128)(2,1)}, u32[]{:S(2)}) copy-start(bf16[256,4,128]{2,0,1:T(8,128)(2,1)} %copy-done.7) | copy-start | bytes 786436
  299.3 368.8 %copy-start.6 = (bf16[256,512]{1,0:T(8,128)(2,1)S(1)}, bf16[256,512]{1,0:T(8,128)(2,1)}, u32[]{:S(2)}) copy-start(bf16[256,512]{1,0:T(8,128)(2,1)} %copy-done.5) | copy-start | bytes 786436
  299.3 412.2 %reduce-scatter.8.cloned.1.call-start = ((), (), s32[]{:S(2)}) async-start(), calls=%async_computation.11 | async-start | bytes 2949120 | tf_op jit(solution)/shard_map/reduce_scatter | solution.py:109
  652.5 61.0 %copy-start.1 = (bf16[4,5120,32]{1,2,0:T(8,128)(2,1)S(1)}, bf16[4,5120,32]{1,2,0:T(8,128)(2,1)}, u32[]{:S(2)}) copy-start(bf16[4,5120,32]{1,2,0:T(8,128)(2,1)} %param.21) | copy-start | bytes 3932164
  667.7 43.8 %copy-start.21 = (f32[1,1,5120]{2,0,1:T(1,128)S(1)}, f32[1,1,5120]{2,0,1:T(1,128)}, u32[]{:S(2)}) copy-start(f32[1,1,5120]{2,0,1:T(1,128)} %get-tuple-element.22) | copy-start | bytes 61444
  667.7 43.8 %copy-start.22 = (f32[1,1,5120]{2,0,1:T(1,128)S(1)}, f32[1,1,5120]{2,0,1:T(1,128)}, u32[]{:S(2)}) copy-start(f32[1,1,5120]{2,0,1:T(1,128)} %get-tuple-element.29) | copy-start | bytes 61444
  667.7 43.8 %copy-start.23 = (f32[1,1,5120]{2,0,1:T(1,128)S(1)}, f32[1,1,5120]{2,0,1:T(1,128)}, u32[]{:S(2)}) copy-start(f32[1,1,5120]{2,0,1:T(1,128)} %get-tuple-element.30) | copy-start | bytes 61444
  667.7 43.9 %copy-start.24 = (f32[1,1,5120]{2,0,1:T(1,128)S(1)}, f32[1,1,5120]{2,0,1:T(1,128)}, u32[]{:S(2)}) copy-start(f32[1,1,5120]{2,0,1:T(1,128)} %get-tuple-element.31) | copy-start | bytes 61444
  669.5 44.0 %copy-start.11 = (bf16[2,16,16,512]{3,2,1,0:T(8,128)(2,1)}, bf16[2,16,16,512]{3,2,1,0:T(8,128)(2,1)S(1)}, u32[]{:S(2)}) copy-start(bf16[2,16,16,512]{3,2,1,0:T(8,128)(2,1)S(1)} %scatter_fusion) | copy-start | bytes 1572868
  (2 other events, 3.6 us)
Sparse Core Ops, SparseCore 0:
  16.3 33.5 all-gather.5
  141.8 43.6 reduce-scatter.3
  188.2 30.0 all-gather.7
  252.9 43.6 reduce-scatter.5
  667.8 43.6 reduce-scatter.7
Sparse Core Ops, SparseCore 1:
  254.8 183.7 all-gather.11
  440.1 181.9 all-gather.13
  624.4 28.1 all-gather.9
where the time goes:
time: 723 us; the launch traced here: 721 us
  waiting for transfers between devices  509 us (70%)
  local copies, waits for them, and re-layouts  61.7 us (9%)
  matrix products  60.8 us (8%)
  blocking collectives  47.6 us (7%)
  other arithmetic  19.5 us (3%)
  between operations  16.2 us (2%)
    all_gather x1, waiting for transfers between devices, body(): lax.all_gather(feedforward_down, 'req', axis=1, tiled=True)  183 us
    all_gather x1, waiting for transfers between devices, body(): lax.all_gather(feedforward_up, 'req', axis=0, tiled=True)  139 us
    reduce_scatter x3, waiting for transfers between devices, sum_rows(): lax.psum_scatter(term_fn(jnp.int32(0), own_count * lax.axis_size('mlp'))....  127 us
    all_gather x3, waiting for transfers between devices, over_group(): lax.all_gather(own_rows, 'mlp', axis=0, tiled=True)  50.2 us
    psum x3, blocking collectives, global_sum(): lax.psum(as_sent(pieces), 'mlp')  47.6 us
    unnamed x85, local copies, waits for them, and re-layouts  30 us
    dot_general x1, matrix products, down_term(): return jnp.dot(hidden, down_full, preferred_element_type=jnp.float32)  15.1 us
  transfers between devices with their start and end apart: 9, of which 8 were waited for; matrix products, arithmetic and copies ran while one was open for 9% of the time, Pallas kernels for 0%

commit v1 on v0

--- a/solution.py
+++ b/solution.py
@@ -7,6 +7,12 @@
 HD = 128
 PAGE = 16
 EPSILON = 1e-06
+
+
+def swap_blocks(shard, axis, split, join):
+    pieces = jnp.split(shard, lax.axis_size(axis), axis=split)
+    received = lax.all_to_all(jnp.stack(pieces), axis, 0, 0)
+    return jnp.concatenate(received, axis=join)
 
 
 def as_sent(array):
@@ -120,9 +126,7 @@
         lax.all_gather(feedforward_up, "req", axis=0, tiled=True),
         lax.all_gather(feedforward_down, "req", axis=1, tiled=True),
     )
-    adapter_up_weight = lax.all_to_all(
-        adapter_up_maps, "mlp", split_axis=3, concat_axis=0, tiled=True
-    )
+    adapter_up_weight = swap_blocks(adapter_up_maps, "mlp", 3, 0)
     slot_total = adapter_up_weight.shape[0]
     bounds = jnp.cumsum(lengths[0])
     position = jnp.arange(group_rows, dtype=jnp.int32)

time: 723 us -> 699 us (0.967)
  local copies, waits for them, and re-layouts: 61.7 us -> 32.8 us
    unnamed x85 -> x91, local copies, waits for them, and re-layouts: 30 us -> 11.2 us
    all_to_all x1 -> x0, local copies, waits for them, and re-layouts: 10.8 us -> none  [body(): lax.all_to_all(adapter_up_maps, 'mlp', split_axis=3, concat_axis=0, tiled...]
  transfers between devices with their start and end apart: 9 -> 9, of which waited for: 8 -> 8; matrix products, arithmetic and copies ran while one was open for 9% -> 5% of each run, Pallas kernels for 0% -> 0%
where the time goes in v1:
time: 699 us; the launch traced here: 698 us
  waiting for transfers between devices  516 us (74%)
  matrix products  59.8 us (9%)
  blocking collectives  48.8 us (7%)
  local copies, waits for them, and re-layouts  32.8 us (5%)
  other arithmetic  18.8 us (3%)
  between operations  16.2 us (2%)
    all_gather x1, waiting for transfers between devices, body(): lax.all_gather(feedforward_down, 'req', axis=1, tiled=True)  183 us
    all_gather x1, waiting for transfers between devices, body(): lax.all_gather(feedforward_up, 'req', axis=0, tiled=True)  139 us
    reduce_scatter x3, waiting for transfers between devices, sum_rows(): lax.psum_scatter(term_fn(jnp.int32(0), own_count * lax.axis_size('mlp'))....  128 us
    all_gather x3, waiting for transfers between devices, over_group(): lax.all_gather(own_rows, 'mlp', axis=0, tiled=True)  50.1 us
    psum x3, blocking collectives, global_sum(): lax.psum(as_sent(pieces), 'mlp')  48.8 us
    dot_general x1, matrix products, down_term(): return jnp.dot(hidden, down_full, preferred_element_type=jnp.float32)  15 us
    all_to_all x1, waiting for transfers between devices, swap_blocks(): received = lax.all_to_all(jnp.stack(pieces), axis, 0, 0)  14.6 us
  transfers between devices with their start and end apart: 9, of which 8 were waited for; matrix products, arithmetic and copies ran while one was open for 5% of the time, Pallas kernels for 0%

profile of v1, /device:TPU:0, one launch (start us, length us, event | category | flops | bytes accessed | tf_op | source)
XLA Modules:
  0.0 698.4 jit_solution(1740659191225537501)
XLA Ops:
  8.1 2.7 fusion.93
  10.8 0.8 reduce-window.8
  11.8 1.1 convert_reduce_fusion.2
  12.9 1.2 fusion.48
  14.2 2.1 fusion.51
  16.3 1.6 bitcast_dynamic-update-slice_fusion.7
  17.8 1.6 bitcast_dynamic-update-slice_fusion.6
  19.4 1.6 bitcast_dynamic-update-slice_fusion.5
  21.0 1.6 bitcast_dynamic-update-slice_fusion.4
  22.5 1.6 bitcast_dynamic-update-slice_fusion.3
  24.1 1.6 bitcast_dynamic-update-slice_fusion.2
  25.7 1.6 bitcast_dynamic-update-slice_fusion.1
  27.2 1.6 bitcast_dynamic-update-slice_fusion
  28.8 5.2 all-to-all-start
  36.1 2.5 compare_select_fusion.10
  39.0 0.8 copy.45
  41.8 14.6 %all-to-all-done = bf16[8,4,2,16,512]{4,3,2,1,0:T(8,128)(2,1)S(1)} async-done(((bf16[8,4,2,16,512]{4,3,2,1,0:T(8,128)(2,1)}), bf16[8,4,2,16,512]{4,3,2,1,0:T(8,128)(2,1)S(1)}, u32[]{:S(2)}, u32[]{:S(2)}) %all-to-all-start) | async-done | bytes 1048608 | tf_op jit(solution)/shard_map/all_to_all | solution.py:14
  56.5 2.7 fusion.99
  59.3 23.9 %psum.28 = bf16[256,32]{0,1:T(8,128)(2,1)S(1)} all-reduce(bf16[256,32]{0,1:T(8,128)(2,1)S(1)} %multiply_reduce_fusion.3), channel_id=1, replica_groups=mesh['req'=4,'mlp'=8] {'mlp'}, use_global_device_ids=true, to_apply=%region_5.6 | all-reduce | flops 8192 | bytes 32768 | tf_op jit(solution)/shard_map/psum | solution.py:123
  83.2 0.8 multiply_convert_fusion.1
  84.0 4.9 fusion.7
  89.4 4.1 multiply_reduce_fusion.1
  93.5 11.8 %all-reduce = (bf16[256]{0:T(256)(128)(2,1)S(1)}, bf16[256]{0:T(256)(128)(2,1)S(1)}) all-reduce(bf16[256]{0:T(256)(128)(2,1)S(1)} %get-tuple-element.62, bf16[256]{0:T(256)(128)(2,1)S(1)} %get-tuple-element.64), channel_id=1, replica_groups=mesh['req'=4,'mlp'=8] {'mlp'}, use_global_device_ids=true, to_apply=%region_9.10 | all-reduce | flops 512 | bytes 2048 | tf_op jit(solution)/shard_map/psum | solution.py:123
  106.7 4.8 fusion.9
  113.4 5.6 convolution_convert_fusion.2
  119.0 1.2 fusion.94
  120.2 43.1 %reduce-scatter.4.cloned.1.call-done = bf16[32,5120]{1,0:T(8,128)(2,1)} async-done(((bf16[256,5120]{1,0:T(8,128)(2,1)}), bf16[32,5120]{1,0:T(8,128)(2,1)}) %reduce-scatter.4.cloned.1.call-update) | async-done | bytes 327696 | tf_op jit(solution)/shard_map/reduce_scatter | solution.py:115
  163.2 1.4 convert_reduce_fusion.1
  164.9 0.9 fusion.47
  166.0 4.0 fusion.89
  170.0 4.0 reshape_squeeze.14
  174.0 2.1 reshape.442
  176.5 19.5 %all-gather.8.cloned.1.call-done = bf16[256,5120]{1,0:T(8,128)(2,1)} async-done(((bf16[32,5120]{1,0:T(8,128)(2,1)}), bf16[256,5120]{1,0:T(8,128)(2,1)}) %all-gather.8.cloned.1.call-update) | async-done | bytes 2621456 | tf_op jit(solution)/shard_map/all_gather | solution.py:112
  196.1 5.6 multiply_reduce_fusion
  201.7 13.1 %psum.31 = bf16[256]{0:T(256)(128)(2,1)S(1)} all-reduce(bf16[256]{0:T(256)(128)(2,1)S(1)} %get-tuple-element.66), channel_id=1, replica_groups=mesh['req'=4,'mlp'=8] {'mlp'}, use_global_device_ids=true, to_apply=%region_15.16 | all-reduce | flops 256 | bytes 1024 | tf_op jit(solution)/shard_map/psum | solution.py:123
  214.8 6.5 fusion
  221.3 5.9 fusion.24
  227.3 3.1 convolution_convert_fusion.1
  231.7 42.6 %reduce-scatter.6.cloned.1.call-done = bf16[32,5120]{1,0:T(8,128)(2,1)} async-done(((bf16[256,5120]{1,0:T(8,128)(2,1)}), bf16[32,5120]{1,0:T(8,128)(2,1)}) %reduce-scatter.6.cloned.1.call-update) | async-done | bytes 327696 | tf_op jit(solution)/shard_map/reduce_scatter | solution.py:115
  274.3 1.2 convert_reduce_fusion
  275.8 1.1 fusion.44
  277.2 139.1 %all-gather.12.cloned.1.call-done = bf16[5120,1024]{1,0:T(8,128)(2,1)} async-done(((bf16[1280,1024]{1,0:T(8,128)(2,1)}), bf16[5120,1024]{1,0:T(8,128)(2,1)}) %all-gather.12.cloned.1.call-update) | async-done | bytes 10485776 | tf_op jit(solution)/shard_map/all_gather | solution.py:126
  416.3 183.4 %all-gather.14.cloned.1.call-done = bf16[1024,5120]{1,0:T(8,128)(2,1)} async-done(((bf16[1024,1280]{1,0:T(8,128)(2,1)}), bf16[1024,5120]{1,0:T(8,128)(2,1)}) %all-gather.14.cloned.1.call-update) | async-done | bytes 10485776 | tf_op jit(solution)/shard_map/all_gather | solution.py:127
  599.7 30.5 %all-gather.10.cloned.1.call-done = bf16[256,5120]{1,0:T(8,128)(2,1)} async-done(((bf16[32,5120]{1,0:T(8,128)(2,1)}), bf16[256,5120]{1,0:T(8,128)(2,1)}) %all-gather.10.cloned.1.call-update) | async-done | bytes 2621456 | tf_op jit(solution)/shard_map/all_gather | solution.py:112
  630.2 15.0 %convolution_convert_fusion = bf16[256,5120]{1,0:T(8,128)(2,1)} fusion(bf16[1024,5120]{1,0:T(8,128)(2,1)} %all-gather.14.cloned.1.call-done, bf16[256,5120]{1,0:T(8,128)(2,1)} %all-gather.10.cloned.1.call-done, bf16[5120,1024]{1,0:T(8,128)(2,1)} %all-gather.12.cloned.1.call-done), kind=kOutput, calls=%fused_computation.6 | convolution fusion | flops 5372379136 | bytes 26214400 | tf_op jit(solution)/shard_map/dot_general | solution.py:258
  645.8 1.2 scatter_fusion
  647.0 42.0 %reduce-scatter.8.cloned.1.call-done = bf16[32,5120]{1,0:T(8,128)(2,1)} async-done(((bf16[256,5120]{1,0:T(8,128)(2,1)}), bf16[32,5120]{1,0:T(8,128)(2,1)}) %reduce-scatter.8.cloned.1.call-update) | async-done | bytes 327696 | tf_op jit(solution)/shard_map/reduce_scatter | solution.py:115
  689.1 2.0 fusion.54
  (156 shorter events, 11.5 us)
Async XLA Ops:
  8.0 48.5 %copy-start = (bf16[4,5120,32]{1,2,0:T(8,128)(2,1)S(1)}, bf16[4,5120,32]{1,2,0:T(8,128)(2,1)}, u32[]{:S(2)}) copy-start(bf16[4,5120,32]{1,2,0:T(8,128)(2,1)} %param.21) | copy-start | bytes 3932164
  8.0 26.0 %copy-start.35 = (s32[3,256]{1,0:T(4,128)S(1)}, s32[3,256]{1,0:T(4,128)}, u32[]{:S(2)}) copy-start(s32[3,256]{1,0:T(4,128)} %param.25) | copy-start | bytes 9220
  8.0 26.1 %copy-start.37 = (s32[4]{0:T(128)S(1)}, s32[4]{0:T(128)}, u32[]{:S(2)}) copy-start(s32[4]{0:T(128)} %param.19) | copy-start | bytes 52
  8.0 26.1 %copy-start.2 = (s32[32]{0:T(128)S(1)}, s32[32]{0:T(128)}, u32[]{:S(2)}) copy-start(s32[32]{0:T(128)} %param.20) | copy-start | bytes 388
  8.0 48.5 %all-gather.6.cloned.1.call-start = ((), (), s32[]{:S(2)}) async-start(), calls=%async_computation.4 | async-start | bytes 2949120 | tf_op jit(solution)/shard_map/all_gather | solution.py:112
  8.1 31.8 %copy-start.34 = (f32[3,512]{1,0:T(4,128)S(1)}, f32[3,512]{1,0:T(4,128)}, u32[]{:S(2)}) copy-start(f32[3,512]{1,0:T(4,128)} %param.24) | copy-start | bytes 18436
  11.8 24.3 %copy-start.30 = (pred[32]{0:T(512)(128)(4,1)}, pred[32]{0:T(512)(128)(4,1)S(1)}, u32[]{:S(2)}) copy-start(pred[32]{0:T(512)(128)(4,1)S(1)} %get-tuple-element.61) | copy-start | bytes 100
  11.8 27.3 %copy-start.28 = (pred[32]{0:T(512)(128)(4,1)}, pred[32]{0:T(512)(128)(4,1)S(1)}, u32[]{:S(2)}) copy-start(pred[32]{0:T(512)(128)(4,1)S(1)} %get-tuple-element.60) | copy-start | bytes 100
  28.8 27.6 %all-to-all-start = ((bf16[8,4,2,16,512]{4,3,2,1,0:T(8,128)(2,1)}), bf16[8,4,2,16,512]{4,3,2,1,0:T(8,128)(2,1)S(1)}, u32[]{:S(2)}, u32[]{:S(2)}) async-start(bf16[8,4,2,16,512]{4,3,2,1,0:T(8,128)(2,1)} %bitcast_dynamic-update-slice_fusion), calls=%async_computation | async-start | bytes 2097152 | tf_op jit(solution)/shard_map/all_to_all | solution.py:14
  34.0 129.2 %reduce-scatter.4.cloned.1.call-start = ((), (), s32[]{:S(2)}) async-start(), calls=%async_computation.5 | async-start | bytes 2949120 | tf_op jit(solution)/shard_map/reduce_scatter | solution.py:115
  56.5 26.7 %copy-start.15 = (f32[256,32]{0,1:T(8,128)S(1)}, f32[256,32]{0,1:T(8,128)}, u32[]{:S(2)}) copy-start(f32[256,32]{0,1:T(8,128)} %fusion.67) | copy-start | bytes 98308
  84.0 5.3 copy-start.4
  89.4 16.0 %copy-start.33 = (f32[1,512]{1,0:T(1,128)S(1)}, f32[1,512]{1,0:T(1,128)}, u32[]{:S(2)}) copy-start(f32[1,512]{1,0:T(1,128)} %get-tuple-element.54) | copy-start | bytes 6148
  93.5 12.5 %copy-start.32 = (f32[1,512]{1,0:T(1,128)S(1)}, f32[1,512]{1,0:T(1,128)}, u32[]{:S(2)}) copy-start(f32[1,512]{1,0:T(1,128)} %get-tuple-element.53) | copy-start | bytes 6148
  106.7 4.9 copy-start.13
  106.7 5.4 copy-start.12
  113.3 49.9 %copy-start.3 = (bf16[32,5120]{1,0:T(8,128)(2,1)S(1)}, bf16[32,5120]{1,0:T(8,128)(2,1)}, u32[]{:S(2)}) copy-start(bf16[32,5120]{1,0:T(8,128)(2,1)} %param.16) | copy-start | bytes 983044
  113.3 49.9 %copy-start.26 = (f32[1,1,5120]{2,0,1:T(1,128)S(1)}, f32[1,1,5120]{2,0,1:T(1,128)}, u32[]{:S(2)}) copy-start(f32[1,1,5120]{2,0,1:T(1,128)} %get-tuple-element.40) | copy-start | bytes 61444
  113.3 49.9 %copy-start.29 = (pred[32]{0:T(512)(128)(4,1)S(1)}, pred[32]{0:T(512)(128)(4,1)}, u32[]{:S(2)}) copy-start(pred[32]{0:T(512)(128)(4,1)} %copy-done.28) | copy-start | bytes 100
  113.3 49.9 %copy-start.31 = (pred[32]{0:T(512)(128)(4,1)S(1)}, pred[32]{0:T(512)(128)(4,1)}, u32[]{:S(2)}) copy-start(pred[32]{0:T(512)(128)(4,1)} %copy-done.30) | copy-start | bytes 100
  118.9 46.0 %copy-start.27 = (f32[5120]{0:T(1024)S(1)}, f32[5120]{0:T(1024)}, u32[]{:S(2)}) copy-start(f32[5120]{0:T(1024)} %param.28) | copy-start | bytes 61444
  119.0 77.1 %all-gather.8.cloned.1.call-start = ((), (), s32[]{:S(2)}) async-start(), calls=%async_computation.6 | async-start | bytes 2949120 | tf_op jit(solution)/shard_map/all_gather | solution.py:112
  165.8 108.4 %reduce-scatter.6.cloned.1.call-start = ((), (), s32[]{:S(2)}) async-start(), calls=%async_computation.7 | async-start | bytes 2949120 | tf_op jit(solution)/shard_map/reduce_scatter | solution.py:115
  176.5 38.3 %copy-start.10 = (bf16[2048,4,128]{2,1,0:T(4,128)(2,1)S(1)}, bf16[2048,4,128]{2,1,0:T(4,128)(2,1)}, u32[]{:S(2)}) copy-start(bf16[2048,4,128]{2,1,0:T(4,128)(2,1)} %reshape_squeeze.14) | copy-start | bytes 6291460
  176.5 38.3 %copy-start.36 = (f32[1,512]{1,0:T(1,128)S(1)}, f32[1,512]{1,0:T(1,128)}, u32[]{:S(2)}) copy-start(f32[1,512]{1,0:T(1,128)} %get-tuple-element.52) | copy-start | bytes 6148
  214.8 6.5 copy-start.9
  214.8 12.4 %slice-start = ((s8[10485760]{0:T(1024)(128)(4,1)}), s8[4194304]{0:T(1024)(128)(4,1)S(1)}, s32[]{:S(2)}) async-start(s8[10485760]{0:T(1024)(128)(4,1)} %bitcast.167), calls=%async_computation.12 | async-start | bytes 8388608
  221.3 5.9 slice-start.1
  221.3 5.9 slice-start.2
  230.4 45.3 %copy-start.16 = (f32[1,1,5120]{2,0,1:T(1,128)S(1)}, f32[1,1,5120]{2,0,1:T(1,128)}, u32[]{:S(2)}) copy-start(f32[1,1,5120]{2,0,1:T(1,128)} %get-tuple-element.23) | copy-start | bytes 61444
  230.4 45.3 %copy-start.17 = (f32[1,1,5120]{2,0,1:T(1,128)S(1)}, f32[1,1,5120]{2,0,1:T(1,128)}, u32[]{:S(2)}) copy-start(f32[1,1,5120]{2,0,1:T(1,128)} %get-tuple-element.24) | copy-start | bytes 61444
  230.4 45.4 %copy-start.18 = (f32[1,1,5120]{2,0,1:T(1,128)S(1)}, f32[1,1,5120]{2,0,1:T(1,128)}, u32[]{:S(2)}) copy-start(f32[1,1,5120]{2,0,1:T(1,128)} %get-tuple-element.25) | copy-start | bytes 61444
  230.4 45.4 %copy-start.19 = (f32[1,1,5120]{2,0,1:T(1,128)S(1)}, f32[1,1,5120]{2,0,1:T(1,128)}, u32[]{:S(2)}) copy-start(f32[1,1,5120]{2,0,1:T(1,128)} %get-tuple-element.26) | copy-start | bytes 61444
  230.4 45.4 %copy-start.20 = (f32[1,1,5120]{2,0,1:T(1,128)S(1)}, f32[1,1,5120]{2,0,1:T(1,128)}, u32[]{:S(2)}) copy-start(f32[1,1,5120]{2,0,1:T(1,128)} %get-tuple-element.27) | copy-start | bytes 61444
  230.4 45.4 %copy-start.21 = (f32[1,1,5120]{2,0,1:T(1,128)S(1)}, f32[1,1,5120]{2,0,1:T(1,128)}, u32[]{:S(2)}) copy-start(f32[1,1,5120]{2,0,1:T(1,128)} %get-tuple-element.28) | copy-start | bytes 61444
  230.4 185.8 %all-gather.12.cloned.1.call-start = ((), (), s32[]{:S(2)}) async-start(), calls=%async_computation.9 | async-start | bytes 13107200 | tf_op jit(solution)/shard_map/all_gather | solution.py:126
  231.0 368.7 %all-gather.14.cloned.1.call-start = ((), (), s32[]{:S(2)}) async-start(), calls=%async_computation.10 | async-start | bytes 13107200 | tf_op jit(solution)/shard_map/all_gather | solution.py:127
  231.6 398.6 %all-gather.10.cloned.1.call-start = ((), (), s32[]{:S(2)}) async-start(), calls=%async_computation.8 | async-start | bytes 2949120 | tf_op jit(solution)/shard_map/all_gather | solution.py:112
  276.9 368.3 %copy-start.38 = (s32[1,16]{1,0:T(1,128)S(1)}, s32[1,16]{1,0:T(1,128)}, u32[]{:S(2)}) copy-start(s32[1,16]{1,0:T(1,128)} %param.26) | copy-start | bytes 196
  276.9 368.3 %copy-start.8 = (bf16[256,4,128]{2,0,1:T(8,128)(2,1)S(1)}, bf16[256,4,128]{2,0,1:T(8,128)(2,1)}, u32[]{:S(2)}) copy-start(bf16[256,4,128]{2,0,1:T(8,128)(2,1)} %copy-done.7) | copy-start | bytes 786436
  276.9 368.7 %copy-start.6 = (bf16[256,512]{1,0:T(8,128)(2,1)S(1)}, bf16[256,512]{1,0:T(8,128)(2,1)}, u32[]{:S(2)}) copy-start(bf16[256,512]{1,0:T(8,128)(2,1)} %copy-done.5) | copy-start | bytes 786436
  277.0 412.1 %reduce-scatter.8.cloned.1.call-start = ((), (), s32[]{:S(2)}) async-start(), calls=%async_computation.11 | async-start | bytes 2949120 | tf_op jit(solution)/shard_map/reduce_scatter | solution.py:115
  645.2 43.9 %copy-start.22 = (f32[1,1,5120]{2,0,1:T(1,128)S(1)}, f32[1,1,5120]{2,0,1:T(1,128)}, u32[]{:S(2)}) copy-start(f32[1,1,5120]{2,0,1:T(1,128)} %get-tuple-element.22) | copy-start | bytes 61444
  645.2 43.9 %copy-start.23 = (f32[1,1,5120]{2,0,1:T(1,128)S(1)}, f32[1,1,5120]{2,0,1:T(1,128)}, u32[]{:S(2)}) copy-start(f32[1,1,5120]{2,0,1:T(1,128)} %get-tuple-element.29) | copy-start | bytes 61444
  645.2 43.9 %copy-start.24 = (f32[1,1,5120]{2,0,1:T(1,128)S(1)}, f32[1,1,5120]{2,0,1:T(1,128)}, u32[]{:S(2)}) copy-start(f32[1,1,5120]{2,0,1:T(1,128)} %get-tuple-element.30) | copy-start | bytes 61444
  645.2 43.9 %copy-start.25 = (f32[1,1,5120]{2,0,1:T(1,128)S(1)}, f32[1,1,5120]{2,0,1:T(1,128)}, u32[]{:S(2)}) copy-start(f32[1,1,5120]{2,0,1:T(1,128)} %get-tuple-element.31) | copy-start | bytes 61444
  645.2 45.8 %copy-start.1 = (bf16[4,5120,32]{1,2,0:T(8,128)(2,1)S(1)}, bf16[4,5120,32]{1,2,0:T(8,128)(2,1)}, u32[]{:S(2)}) copy-start(bf16[4,5120,32]{1,2,0:T(8,128)(2,1)} %param.21) | copy-start | bytes 3932164
  647.0 44.0 %copy-start.11 = (bf16[2,16,16,512]{3,2,1,0:T(8,128)(2,1)}, bf16[2,16,16,512]{3,2,1,0:T(8,128)(2,1)S(1)}, u32[]{:S(2)}) copy-start(bf16[2,16,16,512]{3,2,1,0:T(8,128)(2,1)S(1)} %scatter_fusion) | copy-start | bytes 1572868
  (3 other events, 3.4 us)
Sparse Core Ops, SparseCore 0:
  16.4 39.8 all-gather.5
  119.1 44.0 reduce-scatter.3
  165.9 30.0 all-gather.7
  230.6 43.6 reduce-scatter.5
  645.4 43.6 reduce-scatter.7
Sparse Core Ops, SparseCore 1:
  232.5 183.7 all-gather.11
  417.7 181.9 all-gather.13
  602.0 28.1 all-gather.9
